TPU v7x, 256 devices: a whole 4x4x8 slice. The times are simulated.
256 devices in a mesh: tm: 32 (over z, y), slab: 8 (over x, core).
Axes of the slice: x: 4, y: 4, z: 8, core: 2. Of those that a mesh axis runs over, the one named last changes fastest.
Arguments:
- features: bfloat16 [32, 12288, 256], P('tm', 'slab'), may hold values from -6 to 6
- ref_lists: int32 [32, 8, 32], P('tm'), may hold values from 0 to 11
- tile_rows: int32 [32, 256], P('tm', 'slab'), may hold values from 0 to 11
- tile_sources: int32 [32, 256], P('tm', 'slab'), may hold values from 0 to 31
- tile_counts: int32 [32, 8], P('tm', 'slab'), may hold values from 9 to 32
- tile_values: bfloat16 [32, 256, 128, 128], P('tm', 'slab'), may hold values from -0.3125 to 0.3125
- w_input: bfloat16 [2, 256, 1024], replicated, may hold values from -0.375 to 0.375
- w_hidden: bfloat16 [2, 256, 1024], replicated, may hold values from -0.375 to 0.375
- bias: float32 [2, 1024], replicated, may hold values from -4 to 4
Outputs:
- hidden_out: bfloat16 [32, 12288, 256], P('tm', 'slab')
Inputs may be any that keep to these rules, and one draw needn't show every extreme that they name: `ref_lists`: row tile indices within a slab. `tile_counts`: slots at or after the count are ignored.
All inputs are finite; a program needn't handle non-finite values.
Results may differ from a plain program's by a relative error of at most 0.0055.
Values may be sent and summed in bfloat16 or wider, within the bound.
A program may use at most 64 MiB of HBM per device.

v0:
```python
import jax
import jax.numpy as jnp
from jax import lax
from jax.sharding import PartitionSpec as P


def lstm_run(inputs, weight_in, weight_rec, gate_bias):
    steps_count, vertex_count, feature_width = inputs.shape
    projected = jnp.dot(
        inputs.reshape(-1, feature_width), weight_in, preferred_element_type=jnp.float32
    )
    projected = projected.reshape(steps_count, vertex_count, -1) + gate_bias
    unit_count = weight_rec.shape[0]

    def advance(state, gate_input):
        hidden, memory = state
        gate_sum = gate_input + jnp.dot(hidden, weight_rec, preferred_element_type=jnp.float32)
        in_gate, forget, candidate, out_gate = jnp.split(gate_sum, 4, axis=-1)
        memory = jax.nn.sigmoid(forget) * memory + jax.nn.sigmoid(in_gate) * jnp.tanh(candidate)
        hidden = (jax.nn.sigmoid(out_gate) * jnp.tanh(memory)).astype(jnp.bfloat16)
        return ((hidden, memory), hidden)

    start_state = (
        jnp.zeros((vertex_count, unit_count), jnp.bfloat16),
        jnp.zeros((vertex_count, unit_count), jnp.float32),
    )
    final_state, outputs = lax.scan(advance, start_state, projected, unroll=4)
    return outputs


def local(
    features, ref_lists, tile_rows, tile_sources, tile_counts, tile_values, w_input, w_hidden, bias
):
    current = features[0]
    row_count, feature_width = current.shape
    tile_size = tile_values.shape[2]
    slot_count = tile_values.shape[1]
    row_tiles = row_count // tile_size
    slab_count = lax.axis_size("slab")
    group_count = lax.axis_size("tm")
    slab_index = lax.axis_index("slab")
    ref_table = ref_lists[0]
    list_length = ref_table.shape[1] // slab_count
    weight_tiles = tile_values[0]
    sources = tile_sources[0]
    live = jnp.arange(slot_count, dtype=jnp.int32) < tile_counts[0, 0]
    one_hot = (tile_rows[0][None, :] == jnp.arange(row_tiles, dtype=jnp.int32)[:, None]) & live[
        None, :
    ]
    one_hot = one_hot.astype(jnp.float32)
    for layer_index in range(w_input.shape[0]):
        wanted = lax.dynamic_slice_in_dim(ref_table, slab_index * list_length, list_length, 1)
        own_tiles = current.reshape(row_tiles, tile_size, -1)
        outgoing = jnp.take(own_tiles, wanted.reshape(-1), axis=0).reshape(
            slab_count, list_length, tile_size, -1
        )
        arrived = lax.all_to_all(outgoing, "slab", split_axis=0, concat_axis=0, tiled=True)
        arrived = arrived.reshape(slab_count * list_length, tile_size, -1)
        picked = jnp.take(arrived, sources, axis=0)
        products = jnp.einsum(
            "kij,kjf->kif", weight_tiles, picked, preferred_element_type=jnp.float32
        )
        mixed = jnp.einsum("rk,kif->rif", one_hot, products).astype(jnp.bfloat16)
        grouped = mixed.reshape(group_count, row_count // group_count, -1)

        def recur(vertex_part, layer_index=layer_index):
            states = lstm_run(
                vertex_part, w_input[layer_index], w_hidden[layer_index], bias[layer_index]
            )
            return lax.all_to_all(states, "tm", split_axis=0, concat_axis=0, tiled=True)

        current = recur(
            lax.all_to_all(grouped, "tm", split_axis=0, concat_axis=0, tiled=True)
        ).reshape(row_count, -1)
    return current[None]


def solution(mesh):
    in_specs = (
        P("tm", "slab", None),
        P("tm", None, None),
        P("tm", "slab"),
        P("tm", "slab"),
        P("tm", "slab"),
        P("tm", "slab", None, None),
        P(),
        P(),
        P(),
    )
    out_specs = P("tm", "slab", None)
    return jax.shard_map(local, mesh=mesh, in_specs=in_specs, out_specs=out_specs, check_vma=False)
```

profile of v0, /device:TPU:1, one launch (start us, length us, event | category | flops | bytes accessed | tf_op | source)
XLA Modules:
  0.0 305.5 jit_solution(12780815506039334951)
XLA Ops:
  1.0 3.1 %gather_fusion = bf16[32,128,256]{2,1,0:T(8,128)(2,1)} fusion(bf16[12,128,256]{2,1,0:T(8,128)(2,1)} %bitcast.187, s32[1024]{0:T(1024)S(1)} %pad_clamp_fusion.1), kind=kCustom, calls=%fused_computation.clone | custom fusion | bytes 4194432 | tf_op jit(solution)/shard_map/jit(_take)/gather | solution.py:54
  4.1 3.1 %broadcast_select_fusion = bf16[32,128,256]{2,1,0:T(8,128)(2,1)} fusion(bf16[32,128,256]{2,1,0:T(8,128)(2,1)} %gather_fusion, pred[32]{0:T(512)(128)(4,1)S(1)} %compare_and_fusion.1), kind=kLoop, calls=%fused_computation.188 | loop fusion | flops 1048576 | bytes 4194336 | tf_op jit(solution)/shard_map/jit(_take)/select_n | solution.py:54
  7.2 7.6 %all-to-all-start = ((bf16[8,4,128,256]{3,2,1,0:T(8,128)(2,1)}), bf16[8,4,128,256]{3,2,1,0:T(8,128)(2,1)}, u32[]{:S(2)}, u32[]{:S(2)}) async-start(bf16[8,4,128,256]{3,2,1,0:T(8,128)(2,1)} %bitcast.184), calls=%async_computation | async-start | bytes 4194304 | tf_op jit(solution)/shard_map/all_to_all | solution.py:57
  15.5 25.7 %all-to-all-done = bf16[8,4,128,256]{3,2,1,0:T(8,128)(2,1)} async-done(((bf16[8,4,128,256]{3,2,1,0:T(8,128)(2,1)}), bf16[8,4,128,256]{3,2,1,0:T(8,128)(2,1)}, u32[]{:S(2)}, u32[]{:S(2)}) %all-to-all-start) | async-done | bytes 2097184 | tf_op jit(solution)/shard_map/all_to_all | solution.py:57
  41.3 3.6 %gather_fusion.1 = bf16[32,128,256]{2,1,0:T(8,128)(2,1)} fusion(bf16[32,128,256]{2,1,0:T(8,128)(2,1)} %bitcast.6, s32[1024]{0:T(1024)S(1)} %pad_clamp_fusion), kind=kCustom, calls=%fused_computation.1.clone | custom fusion | bytes 4194432 | tf_op jit(solution)/shard_map/jit(_take)/gather | solution.py:59
  44.9 3.8 %fusion.128 = bf16[32,256,128]{2,1,0:T(8,128)(2,1)} fusion(bf16[32,128,256]{2,1,0:T(8,128)(2,1)} %gather_fusion.1, pred[32]{0:T(512)(128)(4,1)S(1)} %compare_and_fusion, bf16[1,32,128,128]{3,2,1,0:T(8,128)(2,1)S(1)} %copy-done), kind=kOutput, calls=%fused_computation.184 | convolution fusion | flops 269484032 | bytes 5242912 | tf_op jit(solution)/shard_map/kij,kjf->kif/dot_general | solution.py:60
  48.6 4.6 %copy.12 = bf16[32,256,128]{1,0,2:T(8,128)(2,1)} copy(bf16[32,256,128]{2,1,0:T(8,128)(2,1)} %fusion.128) | data formatting | bytes 4194304 | tf_op jit(solution)/shard_map/kij,kjf->kif/dot_general | solution.py:60
  53.2 2.0 fusion.132
  56.3 9.5 %all-to-all-start.1 = ((bf16[32,48,256]{2,1,0:T(8,128)(2,1)}), bf16[32,48,256]{2,1,0:T(8,128)(2,1)S(1)}, u32[]{:S(2)}, u32[]{:S(2)}) async-start(bf16[32,48,256]{2,1,0:T(8,128)(2,1)} %bitcast.194), calls=%async_computation.1 | async-start | bytes 1572864 | tf_op jit(solution)/shard_map/all_to_all | solution.py:73
  65.9 1.3 slice_bitcast_fusion
  67.2 19.7 %all-to-all-done.1 = bf16[32,48,256]{2,1,0:T(8,128)(2,1)S(1)} async-done(((bf16[32,48,256]{2,1,0:T(8,128)(2,1)}), bf16[32,48,256]{2,1,0:T(8,128)(2,1)S(1)}, u32[]{:S(2)}, u32[]{:S(2)}) %all-to-all-start.1) | async-done | bytes 786464 | tf_op jit(solution)/shard_map/all_to_all | solution.py:73
  86.9 4.7 %broadcast_add_fusion.1 = f32[32,48,1024]{2,1,0:T(8,128)} fusion(f32[1024]{0:T(1024)S(1)} %bitcast.201, bf16[32,48,256]{2,1,0:T(8,128)(2,1)S(1)} %all-to-all-done.1, bf16[2,256,1024]{2,1,0:T(8,128)(2,1)} %param.23), kind=kOutput, calls=%fused_computation.181 | convolution fusion | flops 806879232 | bytes 7606272 | tf_op jit(solution)/shard_map/dot_general | solution.py:9
  91.7 39.4 %while.30 = (s32[]{:T(128)}, bf16[48,256]{1,0:T(8,128)(2,1)S(1)}, f32[48,256]{1,0:T(8,128)S(1)}, bf16[8,4,48,256]{3,2,1,0:T(8,128)(2,1)S(1)}, f32[8,4,48,1024]{3...) while((s32[]{:T(128)}, bf16[48,256]{1,0:T(8,128)(2,1)S(1)}, ...), condition=%wide.region_1.0_spmd.clone, body=%wide.region_0.3_spmd.clone.sunk | while | flops 101965824 | bytes 5243068 | solution.py:27
  92.9 1.1 convolution_add_fusion.17
  94.1 1.1 convolution_add_fusion.18
  95.3 1.1 convolution_add_fusion.19
  97.8 1.1 convolution_add_fusion.17
  99.0 1.1 convolution_add_fusion.18
  100.3 1.1 convolution_add_fusion.19
  102.7 1.1 convolution_add_fusion.17
  104.0 1.1 convolution_add_fusion.18
  105.2 1.1 convolution_add_fusion.19
  107.7 1.1 convolution_add_fusion.17
  108.9 1.1 convolution_add_fusion.18
  110.1 1.1 convolution_add_fusion.19
  112.6 1.1 convolution_add_fusion.17
  113.8 1.1 convolution_add_fusion.18
  117.5 1.1 convolution_add_fusion.17
  118.7 1.1 convolution_add_fusion.18
  120.0 1.1 convolution_add_fusion.19
  122.4 1.1 convolution_add_fusion.17
  123.7 1.1 convolution_add_fusion.18
  127.4 1.1 convolution_add_fusion.17
  128.6 1.1 convolution_add_fusion.18
  129.8 1.1 convolution_add_fusion.19
  131.0 25.4 %all_to_all.30 = bf16[32,48,256]{2,1,0:T(8,128)(2,1)S(1)} all-to-all(bf16[32,48,256]{2,1,0:T(8,128)(2,1)S(1)} %bitcast.196), channel_id=1, replica_groups=mesh['tm'=32,'slab'=8] {'tm'}, dimensions={0} | all-to-all | bytes 1572864 | tf_op jit(solution)/shard_map/all_to_all | solution.py:70
  156.5 2.0 gather_fusion.2
  158.5 1.8 broadcast_select_fusion.1
  160.3 33.7 %all_to_all.31 = bf16[8,4,128,256]{3,2,1,0:T(8,128)(2,1)} all-to-all(bf16[8,4,128,256]{3,2,1,0:T(8,128)(2,1)S(1)} %bitcast.185), channel_id=1, replica_groups=mesh['tm'=32,'slab'=8] {'slab'}, dimensions={0} | all-to-all | bytes 4194304 | tf_op jit(solution)/shard_map/all_to_all | solution.py:57
  194.0 3.6 %gather_fusion.3 = bf16[32,128,256]{2,1,0:T(8,128)(2,1)} fusion(bf16[32,128,256]{2,1,0:T(8,128)(2,1)} %bitcast.186, s32[1024]{0:T(1024)S(1)} %pad_clamp_fusion), kind=kCustom, calls=%fused_computation.3.clone | custom fusion | bytes 4194432 | tf_op jit(solution)/shard_map/jit(_take)/gather | solution.py:59
  197.6 3.7 %fusion.126 = bf16[32,256,128]{2,1,0:T(8,128)(2,1)} fusion(bf16[32,128,256]{2,1,0:T(8,128)(2,1)} %gather_fusion.3, pred[32]{0:T(512)(128)(4,1)S(1)} %compare_and_fusion, bf16[1,32,128,128]{3,2,1,0:T(8,128)(2,1)S(1)} %copy-done), kind=kOutput, calls=%fused_computation.182 | convolution fusion | flops 269484032 | bytes 5242912 | tf_op jit(solution)/shard_map/kij,kjf->kif/dot_general | solution.py:60
  201.4 4.6 %copy.13 = bf16[32,256,128]{1,0,2:T(8,128)(2,1)} copy(bf16[32,256,128]{2,1,0:T(8,128)(2,1)} %fusion.126) | data formatting | bytes 4194304 | tf_op jit(solution)/shard_map/kij,kjf->kif/dot_general | solution.py:60
  206.0 2.0 fusion.135
  209.1 4.8 %all-to-all-start.4 = ((bf16[32,48,256]{2,1,0:T(8,128)(2,1)}), bf16[32,48,256]{2,1,0:T(8,128)(2,1)S(1)}, u32[]{:S(2)}, u32[]{:S(2)}) async-start(bf16[32,48,256]{2,1,0:T(8,128)(2,1)} %bitcast.20), calls=%async_computation.4 | async-start | bytes 1572864 | tf_op jit(solution)/shard_map/all_to_all | solution.py:73
  214.0 21.0 %all-to-all-done.4 = bf16[32,48,256]{2,1,0:T(8,128)(2,1)S(1)} async-done(((bf16[32,48,256]{2,1,0:T(8,128)(2,1)}), bf16[32,48,256]{2,1,0:T(8,128)(2,1)S(1)}, u32[]{:S(2)}, u32[]{:S(2)}) %all-to-all-start.4) | async-done | bytes 786464 | tf_op jit(solution)/shard_map/all_to_all | solution.py:73
  235.0 4.7 %broadcast_add_fusion = f32[32,48,1024]{2,1,0:T(8,128)} fusion(f32[1024]{0:T(1024)S(1)} %bitcast.200, bf16[32,48,256]{2,1,0:T(8,128)(2,1)S(1)} %all-to-all-done.4, bf16[2,256,1024]{2,1,0:T(8,128)(2,1)} %param.23), kind=kOutput, calls=%fused_computation.180 | convolution fusion | flops 806879232 | bytes 7606272 | tf_op jit(solution)/shard_map/dot_general | solution.py:9
  239.8 39.4 %while.31 = (s32[]{:T(128)}, bf16[48,256]{1,0:T(8,128)(2,1)S(1)}, f32[48,256]{1,0:T(8,128)S(1)}, bf16[8,4,48,256]{3,2,1,0:T(8,128)(2,1)S(1)}, f32[8,4,48,1024]{3...) while((s32[]{:T(128)}, bf16[48,256]{1,0:T(8,128)(2,1)S(1)}, ...), condition=%wide.region_3.6_spmd.clone, body=%wide.region_2.5_spmd.clone.sunk | while | flops 101965824 | bytes 5243068 | solution.py:27
  241.0 1.1 convolution_add_fusion.21
  242.2 1.1 convolution_add_fusion.22
  243.5 1.1 convolution_add_fusion.23
  247.2 1.1 convolution_add_fusion.22
  250.9 1.1 convolution_add_fusion.21
  252.1 1.1 convolution_add_fusion.22
  253.3 1.1 convolution_add_fusion.23
  257.0 1.1 convolution_add_fusion.22
  260.7 1.1 convolution_add_fusion.21
  261.9 1.1 convolution_add_fusion.22
  263.2 1.1 convolution_add_fusion.23
  266.9 1.1 convolution_add_fusion.22
  270.6 1.1 convolution_add_fusion.21
  271.8 1.1 convolution_add_fusion.22
  273.0 1.1 convolution_add_fusion.23
  276.7 1.1 convolution_add_fusion.22
  279.2 25.4 %all_to_all.32 = bf16[32,48,256]{2,1,0:T(8,128)(2,1)S(1)} all-to-all(bf16[32,48,256]{2,1,0:T(8,128)(2,1)S(1)} %bitcast.195), channel_id=1, replica_groups=mesh['tm'=32,'slab'=8] {'tm'}, dimensions={0} | all-to-all | bytes 1572864 | tf_op jit(solution)/shard_map/all_to_all | solution.py:70
  (133 shorter events, 38.5 us)
Async XLA Ops:
  0.0 44.9 %copy-start = (bf16[1,32,128,128]{3,2,1,0:T(8,128)(2,1)S(1)}, bf16[1,32,128,128]{3,2,1,0:T(8,128)(2,1)}, u32[]{:S(2)}) copy-start(bf16[1,32,128,128]{3,2,1,0:T(8,128)(2,1)} %param.22) | copy-start | bytes 3145732
  7.2 8.3 %copy-start.3 = (s32[1,32]{1,0:T(1,128)S(1)}, s32[1,32]{1,0:T(1,128)}, u32[]{:S(2)}) copy-start(s32[1,32]{1,0:T(1,128)} %param.20) | copy-start | bytes 388
  7.2 34.0 %all-to-all-start = ((bf16[8,4,128,256]{3,2,1,0:T(8,128)(2,1)}), bf16[8,4,128,256]{3,2,1,0:T(8,128)(2,1)}, u32[]{:S(2)}, u32[]{:S(2)}) async-start(bf16[8,4,128,256]{3,2,1,0:T(8,128)(2,1)} %bitcast.184), calls=%async_computation | async-start | bytes 4194304 | tf_op jit(solution)/shard_map/all_to_all | solution.py:57
  48.6 4.6 %copy-start.2 = (s32[1,32]{1,0:T(1,128)S(1)}, s32[1,32]{1,0:T(1,128)}, u32[]{:S(2)}) copy-start(s32[1,32]{1,0:T(1,128)} %param.19) | copy-start | bytes 388
  55.2 10.7 %copy-start.1 = (f32[2,1024]{1,0:T(2,128)S(1)}, f32[2,1024]{1,0:T(2,128)}, u32[]{:S(2)}) copy-start(f32[2,1024]{1,0:T(2,128)} %param.25) | copy-start | bytes 24580
  56.3 30.6 %all-to-all-start.1 = ((bf16[32,48,256]{2,1,0:T(8,128)(2,1)}), bf16[32,48,256]{2,1,0:T(8,128)(2,1)S(1)}, u32[]{:S(2)}, u32[]{:S(2)}) async-start(bf16[32,48,256]{2,1,0:T(8,128)(2,1)} %bitcast.194), calls=%async_computation.1 | async-start | bytes 1572864 | tf_op jit(solution)/shard_map/all_to_all | solution.py:73
  209.1 25.9 %all-to-all-start.4 = ((bf16[32,48,256]{2,1,0:T(8,128)(2,1)}), bf16[32,48,256]{2,1,0:T(8,128)(2,1)S(1)}, u32[]{:S(2)}, u32[]{:S(2)}) async-start(bf16[32,48,256]{2,1,0:T(8,128)(2,1)} %bitcast.20), calls=%async_computation.4 | async-start | bytes 1572864 | tf_op jit(solution)/shard_map/all_to_all | solution.py:73
where the time goes:
time: 310 us; the launch traced here: 305 us
  matrix products  93.7 us (30%)
  blocking collectives  84.5 us (27%)
  waiting for transfers between devices  66.5 us (21%)
  local copies, waits for them, and re-layouts  27 us (9%)
  starting transfers between devices  22 us (7%)
  other arithmetic  9.77 us (3%)
    dot_general x64, matrix products, advance(): jnp.dot(hidden, weight_rec, preferred_element_type=jnp.float32)  72.8 us
    all_to_all x2, blocking collectives, recur(): return lax.all_to_all(states, 'tm', split_axis=0, concat_axis=0, tiled=True)  50.8 us
    all_to_all x2, waiting for transfers between devices, local(): lax.all_to_all(grouped, 'tm', split_axis=0, concat_axis=0, tiled=True)  40.7 us
    all_to_all x1, blocking collectives, local(): lax.all_to_all(outgoing, 'slab', split_axis=0, concat_axis=0, tiled=True)  33.7 us
    all_to_all x1, waiting for transfers between devices, local(): lax.all_to_all(outgoing, 'slab', split_axis=0, concat_axis=0, tiled=True)  25.7 us
    all_to_all x2, starting transfers between devices, local(): lax.all_to_all(grouped, 'tm', split_axis=0, concat_axis=0, tiled=True)  14.4 us
    dot_general x2, matrix products, lstm_run(): jnp.dot(inputs.reshape(-1, feature_width), weight_in, preferred_element_t...  9.37 us
    dot_general x2, local copies, waits for them, and re-layouts, local(): jnp.einsum('kij,kjf->kif', weight_tiles, picked, preferred_element_type=j...  9.17 us
  transfers between devices with their start and end apart: 3, of which 3 were waited for; matrix products, arithmetic and copies ran while one was open for 0% of the time, Pallas kernels for 0%

commit v1 on v0

v1 whole, which is shorter than its diff:
```python
import functools

import jax
import jax.numpy as jnp
from jax import lax
from jax.experimental import pallas as pl
from jax.experimental.pallas import tpu as pltpu
from jax.sharding import PartitionSpec as P

CHUNKS = (16, 32)


def sigmoid(x):
    return 0.5 * jnp.tanh(0.5 * x) + 0.5


def kernel(
    times, slabs, refs, tile, slots, units,
    table, features, values_hbm, w_in_hbm, w_rec_hbm, bias,
    out,
    values, w_in, w_rec, pack, arrived_first, arrived_next, sums, mixed, inputs, hidden, current, gates,
    load_sem, slab_sem, ahead_sem, back_sem,
):
    time, slab = lax.axis_index("tm"), lax.axis_index("slab")
    row_tiles = features.shape[0]
    layers = w_in.shape[0]
    starts = [times * sum(CHUNKS[:n]) for n in range(len(CHUNKS))]
    at_order, at_source, at_keep, at_last, at_filled, at_wanted = (
        0, slots, 2 * slots, 3 * slots, 3 * slots + row_tiles, 3 * slots + 2 * row_tiles,
    )

    loads = [
        pltpu.make_async_copy(values_hbm, values, load_sem.at[0]),
        pltpu.make_async_copy(w_in_hbm, w_in, load_sem.at[1]),
        pltpu.make_async_copy(w_rec_hbm, w_rec, load_sem.at[2]),
    ]
    for load in loads:
        load.start()

    barrier = pltpu.get_barrier_semaphore()

    @pl.loop(1, slabs)
    def _(step):
        pl.semaphore_signal(barrier, device_id={"slab": lax.rem(slab + step, slabs)})

    @pl.loop(1, times)
    def _(step):
        pl.semaphore_signal(barrier, device_id={"tm": lax.rem(time + step, times)})

    pl.semaphore_wait(barrier, slabs - 1 + times - 1)

    def bulk_wait(ref, sem):
        pltpu.make_async_copy(ref, ref, sem).wait()

    for layer in range(layers):
        here = features if layer == 0 else current
        after = out if layer == layers - 1 else current
        arrived = arrived_first if layer % 2 == 0 else arrived_next

        def pack_for(q, target, layer=layer, here=here):
            for j in range(refs):
                target[j] = here[table[at_wanted + q * refs + j]]

        @pl.loop(1, slabs)
        def _(step, layer=layer, pack_for=pack_for, arrived=arrived):
            q = lax.rem(slab + step, slabs)
            pack_for(q, pack.at[layer, q])
            pltpu.make_async_remote_copy(
                src_ref=pack.at[layer, q],
                dst_ref=arrived.at[pl.ds(slab * refs, refs)],
                send_sem=slab_sem.at[layer, 0],
                recv_sem=slab_sem.at[layer, 1],
                device_id={"slab": q},
            ).start()

        pack_for(slab, arrived.at[pl.ds(slab * refs, refs)])
        if layer == 0:
            loads[0].wait()
        bulk_wait(pack.at[layer, pl.ds(0, slabs - 1)], slab_sem.at[layer, 1])

        def add_slot(n, total, arrived=arrived):
            product = jnp.dot(
                values[table[at_order + n]],
                arrived[table[at_source + n]],
                preferred_element_type=jnp.float32,
            )
            total = total * table[at_keep + n].astype(jnp.float32) + product
            sums[n] = total
            return total

        lax.fori_loop(0, slots, add_slot, jnp.zeros((tile, units), jnp.float32))
        for r in range(row_tiles):
            filled = table[at_filled + r].astype(jnp.float32)
            mixed[layer, r * tile : (r + 1) * tile, :] = (
                sums[table[at_last + r]] * filled
            ).astype(jnp.bfloat16)

        for n, (size, start) in enumerate(zip(CHUNKS, starts)):

            @pl.loop(1, times)
            def _(step, n=n, size=size, start=start, layer=layer):
                peer = lax.rem(time + step, times)
                pltpu.make_async_remote_copy(
                    src_ref=mixed.at[layer, pl.ds(start + peer * size, size)],
                    dst_ref=inputs.at[layer, pl.ds(start + time * size, size)],
                    send_sem=ahead_sem.at[layer, n, 0],
                    recv_sem=ahead_sem.at[layer, n, 1],
                    device_id={"tm": peer},
                ).start()

            own = pl.ds(pl.multiple_of(start + time * size, size), size)
            inputs[layer, own, :] = mixed[layer, own, :]

        if layer == 0:
            loads[1].wait()
            loads[2].wait()

        for n, (size, start) in enumerate(zip(CHUNKS, starts)):
            most = (times - 1) * size
            bulk_wait(inputs.at[layer, pl.ds(start, most)], ahead_sem.at[layer, n, 1])

            block = 8 * size

            @pl.loop(0, times // 8)
            def _(m, start=start, block=block, layer=layer):
                part = pl.ds(pl.multiple_of(start + m * block, block), block)
                gates[part, :] = (
                    jnp.dot(inputs[layer, part, :], w_in[layer], preferred_element_type=jnp.float32)
                    + bias[layer : layer + 1, :]
                )

            def advance(t, state, size=size, start=start, layer=layer):
                last, memory = state
                part = pl.ds(pl.multiple_of(start + t * size, size), size)
                total = gates[part, :] + jnp.dot(
                    last, w_rec[layer], preferred_element_type=jnp.float32
                )
                in_gate, forget, candidate, out_gate = (
                    total[:, k * units : (k + 1) * units] for k in range(4)
                )
                memory = sigmoid(forget) * memory + sigmoid(in_gate) * jnp.tanh(candidate)
                last = (sigmoid(out_gate) * jnp.tanh(memory)).astype(jnp.bfloat16)
                hidden[layer, part, :] = last
                return last, memory

            lax.fori_loop(
                0, times, advance,
                (jnp.zeros((size, units), jnp.bfloat16), jnp.zeros((size, units), jnp.float32)),
            )

            home = (start + time * size) // tile
            place = pl.ds(pl.multiple_of(lax.rem(start + time * size, tile), size), size)

            @pl.loop(1, times)
            def _(step, n=n, size=size, start=start, layer=layer, after=after, home=home, place=place):
                peer = lax.rem(time + step, times)
                pltpu.make_async_remote_copy(
                    src_ref=hidden.at[layer, pl.ds(start + peer * size, size)],
                    dst_ref=after.at[home, place],
                    send_sem=back_sem.at[layer, n, 0],
                    recv_sem=back_sem.at[layer, n, 1],
                    device_id={"tm": peer},
                ).start()

            own = pl.ds(pl.multiple_of(start + time * size, size), size)
            after[home, place, :] = hidden[layer, own, :]

        for n, (size, start) in enumerate(zip(CHUNKS, starts)):
            most = (times - 1) * size
            bulk_wait(hidden.at[layer, pl.ds(start, most)], back_sem.at[layer, n, 1])

    for layer in range(layers):
        bulk_wait(pack.at[layer, pl.ds(0, slabs - 1)], slab_sem.at[layer, 0])
        for n, (size, start) in enumerate(zip(CHUNKS, starts)):
            most = (times - 1) * size
            bulk_wait(mixed.at[layer, pl.ds(start, most)], ahead_sem.at[layer, n, 0])
            bulk_wait(hidden.at[layer, pl.ds(start, most)], back_sem.at[layer, n, 0])


def slot_table(wanted, rows, sources, count, row_tiles):
    slots = rows.shape[0]
    index = jnp.arange(slots, dtype=jnp.int32)
    key = jnp.where(index < count, rows, row_tiles)
    before = (key[None, :] < key[:, None]) | (
        (key[None, :] == key[:, None]) & (index[None, :] < index[:, None])
    )
    rank = jnp.sum(before.astype(jnp.int32), axis=1)
    place = (rank[None, :] == index[:, None]).astype(jnp.int32)
    order = jnp.sum(place * index[None, :], axis=1)
    source = jnp.sum(place * sources[None, :], axis=1)
    sorted_key = jnp.sum(place * key[None, :], axis=1)
    keep = jnp.concatenate(
        [jnp.zeros((1,), jnp.int32), (sorted_key[1:] == sorted_key[:-1]).astype(jnp.int32)]
    )
    tiles = jnp.arange(row_tiles, dtype=jnp.int32)[:, None]
    last = jnp.maximum(jnp.sum((key[None, :] <= tiles).astype(jnp.int32), axis=1) - 1, 0)
    filled = jnp.any(key[None, :] == tiles, axis=1).astype(jnp.int32)
    return jnp.concatenate([order, source, keep, last, filled, wanted])


def local(
    features, ref_lists, tile_rows, tile_sources, tile_counts, tile_values, w_input, w_hidden, bias
):
    _, rows, width = features.shape
    _, slots, tile, _ = tile_values.shape
    layers, units = w_hidden.shape[:2]
    slabs, times = lax.axis_size("slab"), lax.axis_size("tm")
    refs = ref_lists.shape[2] // slabs
    wanted = lax.dynamic_slice_in_dim(ref_lists[0], lax.axis_index("slab") * refs, refs, 1)
    table = slot_table(
        wanted.reshape(-1), tile_rows[0], tile_sources[0], tile_counts[0, 0], rows // tile
    )
    vmem = pl.BlockSpec(memory_space=pltpu.VMEM)
    anywhere = pl.BlockSpec(memory_space=pl.ANY)
    parts = len(CHUNKS)
    result = pl.pallas_call(
        functools.partial(kernel, times, slabs, refs, tile, slots, units),
        out_shape=jax.ShapeDtypeStruct((rows // tile, tile, units), jnp.bfloat16),
        in_specs=[
            pl.BlockSpec(memory_space=pltpu.SMEM), vmem, anywhere, anywhere, anywhere, vmem,
        ],
        out_specs=vmem,
        scratch_shapes=[
            pltpu.VMEM(tile_values.shape[1:], jnp.bfloat16),
            pltpu.VMEM(w_input.shape, jnp.bfloat16),
            pltpu.VMEM(w_hidden.shape, jnp.bfloat16),
            pltpu.VMEM((layers, slabs, refs, tile, width), jnp.bfloat16),
            pltpu.VMEM((slabs * refs, tile, width), jnp.bfloat16),
            pltpu.VMEM((slabs * refs, tile, width), jnp.bfloat16),
            pltpu.VMEM((slots, tile, width), jnp.float32),
            pltpu.VMEM((layers, rows, width), jnp.bfloat16),
            pltpu.VMEM((layers, rows, width), jnp.bfloat16),
            pltpu.VMEM((layers, rows, units), jnp.bfloat16),
            pltpu.VMEM((rows // tile, tile, units), jnp.bfloat16),
            pltpu.VMEM((rows, 4 * units), jnp.float32),
            pltpu.SemaphoreType.DMA((3,)),
            pltpu.SemaphoreType.DMA((layers, 2)),
            pltpu.SemaphoreType.DMA((layers, parts, 2)),
            pltpu.SemaphoreType.DMA((layers, parts, 2)),
        ],
        compiler_params=pltpu.CompilerParams(
            collective_id=0, has_side_effects=True, vmem_limit_bytes=56 << 20
        ),
    )(table, features[0].reshape(rows // tile, tile, width), tile_values[0], w_input, w_hidden, bias)
    return result.reshape(1, rows, units)


def solution(mesh):
    in_specs = (
        P("tm", "slab", None),
        P("tm", None, None),
        P("tm", "slab"),
        P("tm", "slab"),
        P("tm", "slab"),
        P("tm", "slab", None, None),
        P(),
        P(),
        P(),
    )
    out_specs = P("tm", "slab", None)
    return jax.shard_map(local, mesh=mesh, in_specs=in_specs, out_specs=out_specs, check_vma=False)
```

time: 310 us -> 153 us (0.49); the launches traced: 305 us -> 152 us
  Pallas kernels: 0 us -> 146 us
  matrix products: 93.7 us -> 0 us
  blocking collectives: 84.5 us -> 0 us
  waiting for transfers between devices: 66.5 us -> 0 us
  local copies, waits for them, and re-layouts: 27 us -> 4.18 us
  starting transfers between devices: 22 us -> 0 us
  other arithmetic: 9.77 us -> 0.65 us
    pallas_call x0 -> x1, Pallas kernels: none -> 146 us  [local(): pl.pallas_call(functools.partial(kernel, times, slabs, refs, tile, slots,...]
    dot_general x70 -> x0, matrix products: 93.7 us -> none  [the longest x64 72.8 us: advance(): jnp.dot(hidden, weight_rec, preferred_element_type=jnp.float32)]
    all_to_all x3 -> x0, blocking collectives: 84.5 us -> none  [the longest x2 50.8 us: recur(): return lax.all_to_all(states, 'tm', split_axis=0, concat_axis=0, tiled=True)]
    all_to_all x3 -> x0, waiting for transfers between devices: 66.5 us -> none  [the longest x2 40.7 us: local(): lax.all_to_all(grouped, 'tm', split_axis=0, concat_axis=0, tiled=True)]
    all_to_all x3 -> x0, starting transfers between devices: 22 us -> none  [the longest x2 14.4 us: local(): lax.all_to_all(grouped, 'tm', split_axis=0, concat_axis=0, tiled=True)]
    gather x4 -> x0, local copies, waits for them, and re-layouts: 12.3 us -> none  [the longest x2 7.18 us: local(): picked = jnp.take(arrived, sources, axis=0)]
    dot_general x2 -> x0, local copies, waits for them, and re-layouts: 9.17 us -> none  [local(): jnp.einsum('kij,kjf->kif', weight_tiles, picked, preferred_element_type=j...]
    select_n x4 -> x1, other arithmetic: 5 us -> 0.01 us  [slot_table(): key = jnp.where(index < count, rows, row_tiles)]
  transfers between devices with their start and end apart: 3 -> 0, of which waited for: 3 -> 0; matrix products, arithmetic and copies ran while one was open for 0% -> 0% of each run, Pallas kernels for 0% -> 0%
where the time goes in v1:
time: 153 us; the launch traced here: 152 us
  Pallas kernels  146 us (95%)
  local copies, waits for them, and re-layouts  4.18 us (3%)
    pallas_call x1, Pallas kernels, local(): pl.pallas_call(functools.partial(kernel, times, slabs, refs, tile, slots,...  146 us
    unnamed x7, local copies, waits for them, and re-layouts  3.36 us

profile of v1, /device:TPU:1, one launch (start us, length us, event | category | flops | bytes accessed | tf_op | source)
XLA Modules:
  0.0 151.9 jit_solution(17912558483486168012)
XLA Ops:
  0.0 0.0 copy-start
  0.7 0.0 copy-start.2
  0.7 0.6 copy-done.2
  1.3 0.2 convert_reduce_fusion
  1.5 0.1 fusion.2
  1.6 0.1 convert_reduce_fusion.1
  1.8 0.0 copy-start.1
  1.8 0.6 copy-done.1
  2.4 0.1 select_reduce_fusion
  2.6 0.1 compare_convert_fusion
  2.6 0.0 copy-done
  2.6 0.1 constant_dynamic-slice_fusion
  2.7 0.1 reshape.25
  2.8 0.7 concatenate.3.table
  3.5 146.4 %shard_map.91 = bf16[12,128,256]{2,1,0:T(8,128)(2,1)} custom-call(s32[152]{0:T(256)} %concatenate.3.table, bf16[12,128,256]{2,1,0:T(8,128)(2,1)} %bitcast.13, bf16[32,128,128]{2,1,0:T(8,128)(2,1)} %bitcast.12, bf16[2,256,1024]{2,1,0:T(8,128)(2,1)} %w_in_hbm.1, bf16[2,256,1024]{2,1,0:T(8,128)(2,1)} %w_rec_hbm.1, f32[2,1024]{1,0:T(2,128)} %bias.1), custom_call_target="tpu_custom_call" | custom-call | tf_op jit(solution)/shard_map/pallas_call | solution.py:216
  149.9 2.1 %copy.12 = bf16[1,1536,256]{2,1,0:T(8,128)(2,1)} copy(bf16[1,1536,256]{2,1,0:T(8,128)(2,1)} %bitcast.11) | data formatting | bytes 1572864
  (4 shorter events, 0.0 us)
Async XLA Ops:
  0.0 2.6 %copy-start = (s32[1,8,32]{2,1,0:T(8,128)S(1)}, s32[1,8,32]{2,1,0:T(8,128)}, u32[]{:S(2)}) copy-start(s32[1,8,32]{2,1,0:T(8,128)} %param.10) | copy-start | bytes 3076
  0.7 0.7 copy-start.2
  1.8 0.7 copy-start.1

commit v2 on v0

v2 whole, which is shorter than its diff:
```python
import functools

import jax
import jax.numpy as jnp
from jax import lax
from jax.experimental import pallas as pl
from jax.experimental.pallas import tpu as pltpu
from jax.sharding import PartitionSpec as P

CHUNKS = (16, 32)
LANES = 128


def sigmoid(x):
    return 0.5 * jnp.tanh(0.5 * x) + 0.5


def bulk_wait(ref, sem):
    pltpu.make_async_copy(ref, ref, sem).wait()


def slot_table(rows, sources, counts, key, rank, order, source, keep, last, filled):
    slots, row_tiles = key.shape[0], last.shape[0]
    count = counts[0, 0]

    @pl.loop(0, slots)
    def _(k):
        key[k] = jnp.where(k < count, rows[0, k], row_tiles) * slots + k

    @pl.loop(0, slots)
    def _(k):
        mine = key[k]
        rank[k] = sum((key[other] < mine).astype(jnp.int32) for other in range(slots))

    @pl.loop(0, slots)
    def _(n):
        slot = sum(jnp.where(rank[k] == n, k, 0) for k in range(slots))
        order[n] = slot
        source[n] = sources[0, slot]
        keep[n] = key[slot] // slots

    @pl.loop(0, row_tiles)
    def _(r):
        ahead = sum((key[k] < (r + 1) * slots).astype(jnp.int32) for k in range(slots))
        below = sum((key[k] < r * slots).astype(jnp.int32) for k in range(slots))
        last[r] = jnp.maximum(ahead - 1, 0)
        filled[r] = (ahead > below).astype(jnp.int32)


def kernel(
    times, slabs, refs,
    rows_hbm, sources_hbm, counts_hbm, lists_hbm, features, values_hbm, w_in_hbm, w_rec_hbm, bias,
    out,
    rows, sources, counts, lists, key, rank, order, source, keep, last_slot, filled,
    values, w_in, w_rec, first0, first1, next0, next1, pack,
    arrived00, arrived01, arrived10, arrived11, sums, mixed, inputs, hidden, final, gates,
    small_sem, load_sem, slab_sem, ahead_sem, back_sem,
):
    time, slab = lax.axis_index("tm"), lax.axis_index("slab")
    slots, row_tiles = key.shape[0], last_slot.shape[0]
    tile = first0.shape[1]
    layers, _, width = w_in.shape
    units = width // 4
    halves = 2
    starts = [times * sum(CHUNKS[:n]) for n in range(len(CHUNKS))]
    chunks = list(enumerate(zip(CHUNKS, starts)))
    current = [[first0, first1], [next0, next1]]
    arrived = [[arrived00, arrived01], [arrived10, arrived11]]

    small = [
        pltpu.make_async_copy(a, b, small_sem.at[n])
        for n, (a, b) in enumerate(
            [(lists_hbm, lists), (rows_hbm, rows), (sources_hbm, sources), (counts_hbm, counts)]
        )
    ]
    loads = [
        pltpu.make_async_copy(a, b, load_sem.at[n])
        for n, (a, b) in enumerate(
            [
                (features.at[:, :, pl.ds(0, LANES)], first0),
                (features.at[:, :, pl.ds(LANES, LANES)], first1),
                (values_hbm, values),
                (w_in_hbm, w_in),
                (w_rec_hbm, w_rec),
            ]
        )
    ]
    for load in small + loads:
        load.start()

    barrier = pltpu.get_barrier_semaphore()

    @pl.loop(1, slabs)
    def _(step):
        pl.semaphore_signal(barrier, device_id={"slab": lax.rem(slab + step, slabs)})

    @pl.loop(1, times)
    def _(step):
        pl.semaphore_signal(barrier, device_id={"tm": lax.rem(time + step, times)})

    small[0].wait()

    def pack_for(layer, half, q, target):
        for j in range(refs):
            target[j] = current[layer][half][lists[0, q, slab * refs + j]]

    def pack_all(layer, half):
        @pl.loop(1, slabs)
        def _(step):
            q = lax.rem(slab + step, slabs)
            pack_for(layer, half, q, pack.at[layer, half, q])

        pack_for(layer, half, slab, arrived[layer][half].at[pl.ds(slab * refs, refs)])

    def send_slab(layer, half):
        @pl.loop(1, slabs)
        def _(step):
            q = lax.rem(slab + step, slabs)
            pltpu.make_async_remote_copy(
                src_ref=pack.at[layer, half, q],
                dst_ref=arrived[layer][half].at[pl.ds(slab * refs, refs)],
                send_sem=slab_sem.at[layer, half, 0],
                recv_sem=slab_sem.at[layer, half, 1],
                device_id={"slab": q},
            ).start()

    def slab_wait(layer, half, end):
        bulk_wait(pack.at[layer, half, pl.ds(0, slabs - 1)], slab_sem.at[layer, half, end])

    def add_slots(layer, half):
        total = jnp.zeros((tile, LANES), jnp.float32)
        for n in range(slots):
            product = jnp.dot(
                values[order[n]],
                arrived[layer][half][source[n]],
                preferred_element_type=jnp.float32,
            )
            if n > 0:
                same = (keep[n] == keep[n - 1]).astype(jnp.int32).astype(jnp.float32)
                product = total * same + product
            total = product
            sums[n] = total
        for r in range(row_tiles):
            live = filled[r].astype(jnp.float32)
            mixed[layer, half, r * tile : (r + 1) * tile, :] = (sums[last_slot[r]] * live).astype(
                jnp.bfloat16
            )

    def send_ahead(layer, half, n, size, start):
        @pl.loop(1, times)
        def _(step):
            peer = lax.rem(time + step, times)
            pltpu.make_async_remote_copy(
                src_ref=mixed.at[layer, half, pl.ds(start + peer * size, size)],
                dst_ref=inputs.at[layer, half, pl.ds(start + time * size, size)],
                send_sem=ahead_sem.at[layer, half, n, 0],
                recv_sem=ahead_sem.at[layer, half, n, 1],
                device_id={"tm": peer},
            ).start()

        own = pl.ds(pl.multiple_of(start + time * size, size), size)
        inputs[layer, half, own, :] = mixed[layer, half, own, :]

    def project(layer, size, start):
        block = 8 * size

        @pl.loop(0, times // 8)
        def _(m):
            part = pl.ds(pl.multiple_of(start + m * block, block), block)
            both = jnp.concatenate([inputs[layer, half, part, :] for half in range(halves)], axis=1)
            gates[part, :] = (
                jnp.dot(both, w_in[layer], preferred_element_type=jnp.float32)
                + bias[layer : layer + 1, :]
            )

    def recur(layer, size, start):
        def advance(t, state):
            before, memory = state
            part = pl.ds(pl.multiple_of(start + t * size, size), size)
            total = gates[part, :] + jnp.dot(
                before, w_rec[layer], preferred_element_type=jnp.float32
            )
            in_gate, forget, candidate, out_gate = (
                total[:, k * units : (k + 1) * units] for k in range(4)
            )
            memory = sigmoid(forget) * memory + sigmoid(in_gate) * jnp.tanh(candidate)
            after = (sigmoid(out_gate) * jnp.tanh(memory)).astype(jnp.bfloat16)
            if layer == layers - 1:
                final[part, :] = after
            else:
                for half in range(halves):
                    hidden[half, part, :] = after[:, half * LANES : (half + 1) * LANES]
            return after, memory

        lax.fori_loop(
            0, times, advance,
            (jnp.zeros((size, units), jnp.bfloat16), jnp.zeros((size, units), jnp.float32)),
            unroll=4,
        )

    def send_back(source_ref, target_ref, sems, size, start):
        home = (start + time * size) // tile
        place = pl.ds(pl.multiple_of(lax.rem(start + time * size, tile), size), size)

        @pl.loop(1, times)
        def _(step):
            peer = lax.rem(time + step, times)
            pltpu.make_async_remote_copy(
                src_ref=source_ref.at[pl.ds(start + peer * size, size)],
                dst_ref=target_ref.at[home, place],
                send_sem=sems.at[0],
                recv_sem=sems.at[1],
                device_id={"tm": peer},
            ).start()

        own = pl.ds(pl.multiple_of(start + time * size, size), size)
        target_ref[home, place, :] = source_ref[own, :]

    most = [pl.ds(start, (times - 1) * size) for _, (size, start) in chunks]

    loads[0].wait()
    pack_all(0, 0)
    pl.semaphore_wait(barrier, slabs - 1 + times - 1)

    for layer in range(layers):
        send_slab(layer, 0)
        if layer == 0:
            loads[1].wait()
        else:
            for n, _ in chunks:
                bulk_wait(hidden.at[1, most[n]], back_sem.at[layer - 1, 1, n, 1])
        pack_all(layer, 1)
        slab_wait(layer, 0, 0)
        send_slab(layer, 1)
        if layer == 0:
            for load in small[1:]:
                load.wait()
            slot_table(
                rows, sources, counts, key, rank, order, source, keep, last_slot, filled
            )
            loads[2].wait()

        for half in range(halves):
            slab_wait(layer, half, 1)
            add_slots(layer, half)
            for n, (size, start) in chunks:
                send_ahead(layer, half, n, size, start)

        if layer == 0:
            loads[3].wait()
            loads[4].wait()

        for n, (size, start) in chunks:
            for half in range(halves):
                bulk_wait(inputs.at[layer, half, most[n]], ahead_sem.at[layer, half, n, 1])
            project(layer, size, start)
            recur(layer, size, start)
            if layer == layers - 1:
                send_back(final, out, back_sem.at[layer, 0, n], size, start)
            else:
                for half in range(halves):
                    send_back(
                        hidden.at[half], current[layer + 1][half], back_sem.at[layer, half, n], size, start
                    )

        if layer == layers - 1:
            for n, _ in chunks:
                bulk_wait(final.at[most[n]], back_sem.at[layer, 0, n, 1])
        else:
            for n, _ in chunks:
                bulk_wait(hidden.at[0, most[n]], back_sem.at[layer, 0, n, 1])
            pack_all(layer + 1, 0)

    for layer in range(layers):
        slab_wait(layer, 1, 0)
        for n, _ in chunks:
            for half in range(halves):
                bulk_wait(mixed.at[layer, half, most[n]], ahead_sem.at[layer, half, n, 0])
            if layer == layers - 1:
                bulk_wait(final.at[most[n]], back_sem.at[layer, 0, n, 0])
            else:
                for half in range(halves):
                    bulk_wait(hidden.at[half, most[n]], back_sem.at[layer, half, n, 0])


def local(
    features, ref_lists, tile_rows, tile_sources, tile_counts, tile_values, w_input, w_hidden, bias
):
    _, rows, width = features.shape
    _, slots, tile, _ = tile_values.shape
    layers, units = w_hidden.shape[:2]
    slabs, times = lax.axis_size("slab"), lax.axis_size("tm")
    refs = ref_lists.shape[2] // slabs
    row_tiles, listed, halves, parts = rows // tile, slabs * refs, width // LANES, len(CHUNKS)
    vmem = pl.BlockSpec(memory_space=pltpu.VMEM)
    anywhere = pl.BlockSpec(memory_space=pl.ANY)
    narrow = pltpu.VMEM((row_tiles, tile, LANES), jnp.bfloat16)
    landing = pltpu.VMEM((listed, tile, LANES), jnp.bfloat16)
    half_rows = pltpu.VMEM((layers, halves, rows, LANES), jnp.bfloat16)
    result = pl.pallas_call(
        functools.partial(kernel, times, slabs, refs),
        out_shape=jax.ShapeDtypeStruct((row_tiles, tile, units), jnp.bfloat16),
        in_specs=[anywhere] * 8 + [vmem],
        out_specs=vmem,
        scratch_shapes=[
            pltpu.SMEM(tile_rows.shape, jnp.int32),
            pltpu.SMEM(tile_sources.shape, jnp.int32),
            pltpu.SMEM(tile_counts.shape, jnp.int32),
            pltpu.SMEM(ref_lists.shape, jnp.int32),
            *[pltpu.SMEM((slots,), jnp.int32)] * 5,
            *[pltpu.SMEM((row_tiles,), jnp.int32)] * 2,
            pltpu.VMEM(tile_values.shape[1:], jnp.bfloat16),
            pltpu.VMEM(w_input.shape, jnp.bfloat16),
            pltpu.VMEM(w_hidden.shape, jnp.bfloat16),
            *[narrow] * 4,
            pltpu.VMEM((layers, halves, slabs, refs, tile, LANES), jnp.bfloat16),
            *[landing] * 4,
            pltpu.VMEM((slots, tile, LANES), jnp.float32),
            half_rows,
            half_rows,
            pltpu.VMEM((halves, rows, LANES), jnp.bfloat16),
            pltpu.VMEM((rows, units), jnp.bfloat16),
            pltpu.VMEM((rows, 4 * units), jnp.float32),
            pltpu.SemaphoreType.DMA((4,)),
            pltpu.SemaphoreType.DMA((5,)),
            pltpu.SemaphoreType.DMA((layers, halves, 2)),
            pltpu.SemaphoreType.DMA((layers, halves, parts, 2)),
            pltpu.SemaphoreType.DMA((layers, halves, parts, 2)),
        ],
        compiler_params=pltpu.CompilerParams(
            collective_id=0, has_side_effects=True, vmem_limit_bytes=56 << 20
        ),
    )(
        tile_rows, tile_sources, tile_counts, ref_lists,
        features[0].reshape(row_tiles, tile, width), tile_values[0], w_input, w_hidden, bias,
    )
    return result.reshape(1, rows, units)


def solution(mesh):
    in_specs = (
        P("tm", "slab", None),
        P("tm", None, None),
        P("tm", "slab"),
        P("tm", "slab"),
        P("tm", "slab"),
        P("tm", "slab", None, None),
        P(),
        P(),
        P(),
    )
    out_specs = P("tm", "slab", None)
    return jax.shard_map(local, mesh=mesh, in_specs=in_specs, out_specs=out_specs, check_vma=False)
```

time: 310 us -> 136 us (0.44); the launches traced: 305 us -> 136 us
  Pallas kernels: 0 us -> 133 us
  matrix products: 93.7 us -> 0 us
  blocking collectives: 84.5 us -> 0 us
  waiting for transfers between devices: 66.5 us -> 0 us
  local copies, waits for them, and re-layouts: 27 us -> 2.06 us
  starting transfers between devices: 22 us -> 0 us
  other arithmetic: 9.77 us -> 0 us
    pallas_call x0 -> x1, Pallas kernels: none -> 133 us  [local(): pl.pallas_call(functools.partial(kernel, times, slabs, refs), out_shape=j...]
    dot_general x70 -> x0, matrix products: 93.7 us -> none  [the longest x64 72.8 us: advance(): jnp.dot(hidden, weight_rec, preferred_element_type=jnp.float32)]
    all_to_all x3 -> x0, blocking collectives: 84.5 us -> none  [the longest x2 50.8 us: recur(): return lax.all_to_all(states, 'tm', split_axis=0, concat_axis=0, tiled=True)]
    all_to_all x3 -> x0, waiting for transfers between devices: 66.5 us -> none  [the longest x2 40.7 us: local(): lax.all_to_all(grouped, 'tm', split_axis=0, concat_axis=0, tiled=True)]
    all_to_all x3 -> x0, starting transfers between devices: 22 us -> none  [the longest x2 14.4 us: local(): lax.all_to_all(grouped, 'tm', split_axis=0, concat_axis=0, tiled=True)]
    gather x4 -> x0, local copies, waits for them, and re-layouts: 12.3 us -> none  [the longest x2 7.18 us: local(): picked = jnp.take(arrived, sources, axis=0)]
    dot_general x2 -> x0, local copies, waits for them, and re-layouts: 9.17 us -> none  [local(): jnp.einsum('kij,kjf->kif', weight_tiles, picked, preferred_element_type=j...]
    select_n x4 -> x0, other arithmetic: 5 us -> none  [the longest x3 4.99 us: local(): jnp.take(own_tiles, wanted.reshape(-1), axis=0)]
  transfers between devices with their start and end apart: 3 -> 0, of which waited for: 3 -> 0; matrix products, arithmetic and copies ran while one was open for 0% -> 0% of each run, Pallas kernels for 0% -> 0%
where the time goes in v2:
time: 136 us
  Pallas kernels  133 us (98%)
  local copies, waits for them, and re-layouts  2.06 us (2%)
    pallas_call x1, Pallas kernels, local(): pl.pallas_call(functools.partial(kernel, times, slabs, refs), out_shape=j...  133 us

profile of v2, /device:TPU:1, one launch (start us, length us, event | category | flops | bytes accessed | tf_op | source)
XLA Modules:
  0.0 135.5 jit_solution(13291180497689735428)
XLA Ops:
  0.7 132.8 %shard_map.91 = bf16[12,128,256]{2,1,0:T(8,128)(2,1)} custom-call(s32[1,32]{1,0:T(1,128)} %rows_hbm.1, s32[1,32]{1,0:T(1,128)} %sources_hbm.1, s32[1,1]{1,0:T(1,128)S(6)} %copy.11.counts_hbm, s32[1,8,32]{2,1,0:T(8,128)} %lists_hbm.1, bf16[12,128,256]{2,1,0:T(8,128)(2,1)} %bitcast.5, bf16[32,128,128]{2,1,0:T(8,128)(2,1)} %bitcast.4, ...), custom_call_target="tpu_custom_call" | custom-call | tf_op jit(solution)/shard_map/pallas_call | solution.py:300
  133.5 2.1 %copy.12 = bf16[1,1536,256]{2,1,0:T(8,128)(2,1)} copy(bf16[1,1536,256]{2,1,0:T(8,128)(2,1)} %bitcast.3) | data formatting | bytes 1572864

commit v3 on v2

--- a/solution.py
+++ b/solution.py
@@ -7,7 +7,9 @@
 from jax.experimental.pallas import tpu as pltpu
 from jax.sharding import PartitionSpec as P
 
-CHUNKS = (16, 32)
+CHUNKS = ((16, 32), (16, 32))
+BURST = 4
+SMALL = 16
 LANES = 128
 
 
@@ -49,10 +51,10 @@
 
 def kernel(
     times, slabs, refs,
-    rows_hbm, sources_hbm, counts_hbm, lists_hbm, features, values_hbm, w_in_hbm, w_rec_hbm, bias,
+    rows_hbm, sources_hbm, counts_hbm, lists_hbm, features, values_hbm, w_in_hbm, w_rec_hbm, bias_hbm,
     out,
     rows, sources, counts, lists, key, rank, order, source, keep, last_slot, filled,
-    values, w_in, w_rec, first0, first1, next0, next1, pack,
+    values, w_in, w_rec, bias, first0, first1, next0, next1, pack,
     arrived00, arrived01, arrived10, arrived11, sums, mixed, inputs, hidden, final, gates,
     small_sem, load_sem, slab_sem, ahead_sem, back_sem,
 ):
@@ -62,8 +64,8 @@
     layers, _, width = w_in.shape
     units = width // 4
     halves = 2
-    starts = [times * sum(CHUNKS[:n]) for n in range(len(CHUNKS))]
-    chunks = list(enumerate(zip(CHUNKS, starts)))
+    parts = [len(sizes) for sizes in CHUNKS]
+    starts = [[times * sum(sizes[:n]) for n in range(len(sizes))] for sizes in CHUNKS]
     current = [[first0, first1], [next0, next1]]
     arrived = [[arrived00, arrived01], [arrived10, arrived11]]
 
@@ -82,6 +84,7 @@
                 (values_hbm, values),
                 (w_in_hbm, w_in),
                 (w_rec_hbm, w_rec),
+                (bias_hbm, bias),
             ]
         )
     ]
@@ -113,8 +116,7 @@
         pack_for(layer, half, slab, arrived[layer][half].at[pl.ds(slab * refs, refs)])
 
     def send_slab(layer, half):
-        @pl.loop(1, slabs)
-        def _(step):
+        for step in range(1, slabs):
             q = lax.rem(slab + step, slabs)
             pltpu.make_async_remote_copy(
                 src_ref=pack.at[layer, half, q],
@@ -146,40 +148,54 @@
                 jnp.bfloat16
             )
 
-    def send_ahead(layer, half, n, size, start):
+    def rows_of(layer, n, device):
+        size, start = CHUNKS[layer][n], starts[layer][n]
+        return pl.ds(pl.multiple_of(start + device * size, size), size)
+
+    def every_peer(send):
         @pl.loop(1, times)
         def _(step):
-            peer = lax.rem(time + step, times)
+            send(lax.rem(time + step, times))
+
+    def send_ahead(layer, half, n):
+        def send(peer):
             pltpu.make_async_remote_copy(
-                src_ref=mixed.at[layer, half, pl.ds(start + peer * size, size)],
-                dst_ref=inputs.at[layer, half, pl.ds(start + time * size, size)],
+                src_ref=mixed.at[layer, half, rows_of(layer, n, peer)],
+                dst_ref=inputs.at[layer, half, rows_of(layer, n, time)],
                 send_sem=ahead_sem.at[layer, half, n, 0],
                 recv_sem=ahead_sem.at[layer, half, n, 1],
                 device_id={"tm": peer},
             ).start()
 
-        own = pl.ds(pl.multiple_of(start + time * size, size), size)
-        inputs[layer, half, own, :] = mixed[layer, half, own, :]
-
-    def project(layer, size, start):
+        return send
+
+    def keep_own(layer, half, n):
+        inputs[layer, half, rows_of(layer, n, time), :] = mixed[layer, half, rows_of(layer, n, time), :]
+
+    def projected(layer, part):
+        both = jnp.concatenate([inputs[layer, half, part, :] for half in range(halves)], axis=1)
+        return (
+            jnp.dot(both, w_in[layer], preferred_element_type=jnp.float32)
+            + bias[layer : layer + 1, :]
+        )
+
+    def project(layer, n):
+        size, start = CHUNKS[layer][n], starts[layer][n]
         block = 8 * size
 
         @pl.loop(0, times // 8)
         def _(m):
             part = pl.ds(pl.multiple_of(start + m * block, block), block)
-            both = jnp.concatenate([inputs[layer, half, part, :] for half in range(halves)], axis=1)
-            gates[part, :] = (
-                jnp.dot(both, w_in[layer], preferred_element_type=jnp.float32)
-                + bias[layer : layer + 1, :]
-            )
-
-    def recur(layer, size, start):
+            gates[part, :] = projected(layer, part)
+
+    def recur(layer, n, send=None):
+        size = CHUNKS[layer][n]
+
         def advance(t, state):
             before, memory = state
-            part = pl.ds(pl.multiple_of(start + t * size, size), size)
-            total = gates[part, :] + jnp.dot(
-                before, w_rec[layer], preferred_element_type=jnp.float32
-            )
+            part = rows_of(layer, n, t)
+            total = projected(layer, part) if size <= SMALL else gates[part, :]
+            total = total + jnp.dot(before, w_rec[layer], preferred_element_type=jnp.float32)
             in_gate, forget, candidate, out_gate = (
                 total[:, k * units : (k + 1) * units] for k in range(4)
             )
@@ -192,45 +208,69 @@
                     hidden[half, part, :] = after[:, half * LANES : (half + 1) * LANES]
             return after, memory
 
-        lax.fori_loop(
-            0, times, advance,
-            (jnp.zeros((size, units), jnp.bfloat16), jnp.zeros((size, units), jnp.float32)),
-            unroll=4,
-        )
-
-    def send_back(source_ref, target_ref, sems, size, start):
-        home = (start + time * size) // tile
-        place = pl.ds(pl.multiple_of(lax.rem(start + time * size, tile), size), size)
-
-        @pl.loop(1, times)
-        def _(step):
-            peer = lax.rem(time + step, times)
+        zero = (jnp.zeros((size, units), jnp.bfloat16), jnp.zeros((size, units), jnp.float32))
+        if send is None:
+            lax.fori_loop(0, times, advance, zero, unroll=8)
+            return
+
+        def burst(m, state):
+            for k in range(BURST):
+                state = advance(m * BURST + k, state)
+            for k in range(1, BURST):
+                send(m * BURST + lax.rem(time + k, BURST))
+
+            @pl.when(m != time // BURST)
+            def _():
+                send(m * BURST + lax.rem(time, BURST))
+
+            return state
+
+        lax.fori_loop(0, times // BURST, burst, zero)
+
+    def returned(layer, half):
+        if layer == layers - 1:
+            return final, out
+        return hidden.at[half], current[layer + 1][half]
+
+    def send_back(layer, half, n):
+        kept, target = returned(layer, half)
+        row = starts[layer][n] + time * CHUNKS[layer][n]
+        place = pl.ds(pl.multiple_of(lax.rem(row, tile), CHUNKS[layer][n]), CHUNKS[layer][n])
+
+        def send(peer):
             pltpu.make_async_remote_copy(
-                src_ref=source_ref.at[pl.ds(start + peer * size, size)],
-                dst_ref=target_ref.at[home, place],
-                send_sem=sems.at[0],
-                recv_sem=sems.at[1],
+                src_ref=kept.at[rows_of(layer, n, peer)],
+                dst_ref=target.at[row // tile, place],
+                send_sem=back_sem.at[layer, half, n, 0],
+                recv_sem=back_sem.at[layer, half, n, 1],
                 device_id={"tm": peer},
             ).start()
 
-        own = pl.ds(pl.multiple_of(start + time * size, size), size)
-        target_ref[home, place, :] = source_ref[own, :]
-
-    most = [pl.ds(start, (times - 1) * size) for _, (size, start) in chunks]
+        return send
+
+    def return_own(layer, half, n):
+        kept, target = returned(layer, half)
+        row = starts[layer][n] + time * CHUNKS[layer][n]
+        place = pl.ds(pl.multiple_of(lax.rem(row, tile), CHUNKS[layer][n]), CHUNKS[layer][n])
+        target[row // tile, place, :] = kept[rows_of(layer, n, time), :]
+
+    def peers_bytes(layer, n):
+        return pl.ds(starts[layer][n], (times - 1) * CHUNKS[layer][n])
 
     loads[0].wait()
     pack_all(0, 0)
     pl.semaphore_wait(barrier, slabs - 1 + times - 1)
 
     for layer in range(layers):
+        back_halves = range(1 if layer == layers - 1 else halves)
+        final_part = parts[layer] - 1
         send_slab(layer, 0)
         if layer == 0:
             loads[1].wait()
         else:
-            for n, _ in chunks:
-                bulk_wait(hidden.at[1, most[n]], back_sem.at[layer - 1, 1, n, 1])
+            for n in range(parts[layer - 1]):
+                bulk_wait(hidden.at[1, peers_bytes(layer - 1, n)], back_sem.at[layer - 1, 1, n, 1])
         pack_all(layer, 1)
-        slab_wait(layer, 0, 0)
         send_slab(layer, 1)
         if layer == 0:
             for load in small[1:]:
@@ -238,49 +278,52 @@
             slot_table(
                 rows, sources, counts, key, rank, order, source, keep, last_slot, filled
             )
-            loads[2].wait()
+            for load in loads[2:]:
+                load.wait()
 
         for half in range(halves):
             slab_wait(layer, half, 1)
             add_slots(layer, half)
-            for n, (size, start) in chunks:
-                send_ahead(layer, half, n, size, start)
-
-        if layer == 0:
-            loads[3].wait()
-            loads[4].wait()
-
-        for n, (size, start) in chunks:
+            for n in range(parts[layer]):
+                every_peer(send_ahead(layer, half, n))
+                keep_own(layer, half, n)
+
+        for n in range(parts[layer]):
             for half in range(halves):
-                bulk_wait(inputs.at[layer, half, most[n]], ahead_sem.at[layer, half, n, 1])
-            project(layer, size, start)
-            recur(layer, size, start)
+                bulk_wait(inputs.at[layer, half, peers_bytes(layer, n)], ahead_sem.at[layer, half, n, 1])
+            if CHUNKS[layer][n] > SMALL:
+                project(layer, n)
+            if n < final_part:
+                recur(layer, n)
+                for half in back_halves:
+                    every_peer(send_back(layer, half, n))
+            else:
+                recur(layer, n, send_back(layer, 0, n))
+            for half in back_halves:
+                return_own(layer, half, n)
+
+        if layer == layers - 1:
+            for n in range(parts[layer]):
+                bulk_wait(final.at[peers_bytes(layer, n)], back_sem.at[layer, 0, n, 1])
+        else:
+            bulk_wait(hidden.at[0, peers_bytes(layer, final_part)], back_sem.at[layer, 0, final_part, 0])
+            every_peer(send_back(layer, 1, final_part))
+            for n in range(parts[layer]):
+                bulk_wait(hidden.at[0, peers_bytes(layer, n)], back_sem.at[layer, 0, n, 1])
+            pack_all(layer + 1, 0)
+
+    for layer in range(layers):
+        for half in range(halves):
+            slab_wait(layer, half, 0)
+        for n in range(parts[layer]):
+            for half in range(halves):
+                bulk_wait(mixed.at[layer, half, peers_bytes(layer, n)], ahead_sem.at[layer, half, n, 0])
             if layer == layers - 1:
-                send_back(final, out, back_sem.at[layer, 0, n], size, start)
+                bulk_wait(final.at[peers_bytes(layer, n)], back_sem.at[layer, 0, n, 0])
             else:
                 for half in range(halves):
-                    send_back(
-                        hidden.at[half], current[layer + 1][half], back_sem.at[layer, half, n], size, start
-                    )
-
-        if layer == layers - 1:
-            for n, _ in chunks:
-                bulk_wait(final.at[most[n]], back_sem.at[layer, 0, n, 1])
-        else:
-            for n, _ in chunks:
-                bulk_wait(hidden.at[0, most[n]], back_sem.at[layer, 0, n, 1])
-            pack_all(layer + 1, 0)
-
-    for layer in range(layers):
-        slab_wait(layer, 1, 0)
-        for n, _ in chunks:
-            for half in range(halves):
-                bulk_wait(mixed.at[layer, half, most[n]], ahead_sem.at[layer, half, n, 0])
-            if layer == layers - 1:
-                bulk_wait(final.at[most[n]], back_sem.at[layer, 0, n, 0])
-            else:
-                for half in range(halves):
-                    bulk_wait(hidden.at[half, most[n]], back_sem.at[layer, half, n, 0])
+                    if n < parts[layer] - 1 or half > 0:
+                        bulk_wait(hidden.at[half, peers_bytes(layer, n)], back_sem.at[layer, half, n, 0])
 
 
 def local(
@@ -291,16 +334,17 @@
     layers, units = w_hidden.shape[:2]
     slabs, times = lax.axis_size("slab"), lax.axis_size("tm")
     refs = ref_lists.shape[2] // slabs
-    row_tiles, listed, halves, parts = rows // tile, slabs * refs, width // LANES, len(CHUNKS)
+    row_tiles, listed, halves = rows // tile, slabs * refs, width // LANES
+    parts = max(len(sizes) for sizes in CHUNKS)
     vmem = pl.BlockSpec(memory_space=pltpu.VMEM)
-    anywhere = pl.BlockSpec(memory_space=pl.ANY)
+    far = pl.BlockSpec(memory_space=pltpu.HBM)
     narrow = pltpu.VMEM((row_tiles, tile, LANES), jnp.bfloat16)
     landing = pltpu.VMEM((listed, tile, LANES), jnp.bfloat16)
     half_rows = pltpu.VMEM((layers, halves, rows, LANES), jnp.bfloat16)
     result = pl.pallas_call(
         functools.partial(kernel, times, slabs, refs),
         out_shape=jax.ShapeDtypeStruct((row_tiles, tile, units), jnp.bfloat16),
-        in_specs=[anywhere] * 8 + [vmem],
+        in_specs=[far] * 9,
         out_specs=vmem,
         scratch_shapes=[
             pltpu.SMEM(tile_rows.shape, jnp.int32),
@@ -312,6 +356,7 @@
             pltpu.VMEM(tile_values.shape[1:], jnp.bfloat16),
             pltpu.VMEM(w_input.shape, jnp.bfloat16),
             pltpu.VMEM(w_hidden.shape, jnp.bfloat16),
+            pltpu.VMEM(bias.shape, jnp.float32),
             *[narrow] * 4,
             pltpu.VMEM((layers, halves, slabs, refs, tile, LANES), jnp.bfloat16),
             *[landing] * 4,
@@ -322,13 +367,13 @@
             pltpu.VMEM((rows, units), jnp.bfloat16),
             pltpu.VMEM((rows, 4 * units), jnp.float32),
             pltpu.SemaphoreType.DMA((4,)),
-            pltpu.SemaphoreType.DMA((5,)),
+            pltpu.SemaphoreType.DMA((6,)),
             pltpu.SemaphoreType.DMA((layers, halves, 2)),
             pltpu.SemaphoreType.DMA((layers, halves, parts, 2)),
             pltpu.SemaphoreType.DMA((layers, halves, parts, 2)),
         ],
         compiler_params=pltpu.CompilerParams(
-            collective_id=0, has_side_effects=True, vmem_limit_bytes=56 << 20
+            collective_id=0, has_side_effects=True, vmem_limit_bytes=52 << 20
         ),
     )(
         tile_rows, tile_sources, tile_counts, ref_lists,

time: 136 us -> 123 us (0.904)
  Pallas kernels: 133 us -> 118 us
    pallas_call x1, Pallas kernels: 133 us -> 118 us  [local(): pl.pallas_call(functools.partial(kernel, times, slabs, refs), out_shape=j...]
    unnamed x1 -> x11, local copies, waits for them, and re-layouts: 2.06 us -> 3.36 us
where the time goes in v3:
time: 123 us; the launch traced here: 122 us
  Pallas kernels  118 us (96%)
  local copies, waits for them, and re-layouts  3.36 us (3%)
    pallas_call x1, Pallas kernels, local(): pl.pallas_call(functools.partial(kernel, times, slabs, refs), out_shape=j...  118 us
    unnamed x11, local copies, waits for them, and re-layouts  3.36 us

profile of v3, /device:TPU:1, one launch (start us, length us, event | category | flops | bytes accessed | tf_op | source)
XLA Modules:
  0.0 122.1 jit_solution(6247648295837982208)
XLA Ops:
  0.0 0.0 copy-start.2
  0.7 0.0 copy-start.3
  0.7 0.0 copy-start.4
  0.7 0.0 copy-done.2
  0.7 0.6 copy-done.3
  1.3 0.0 copy-done.4
  1.3 0.0 copy-start
  1.3 1.1 copy-done
  2.5 0.0 copy-start.1
  2.5 0.7 copy-done.1
  3.2 118.0 %shard_map.91 = bf16[12,128,256]{2,1,0:T(8,128)(2,1)S(1)} custom-call(s32[1,32]{1,0:T(1,128)S(1)} %copy-done.3, s32[1,32]{1,0:T(1,128)S(1)} %copy-done.4, s32[1,1]{1,0:T(1,128)S(6)} %copy.11.counts_hbm, s32[1,8,32]{2,1,0:T(8,128)S(1)} %copy-done.2, bf16[12,128,256]{2,1,0:T(8,128)(2,1)S(1)} %bitcast.4, bf16[32,128,128]{2,1,0:T(8,128)(2,1)} %bitcast.5, ...), custom_call_target="tpu_custom_call" | custom-call | tf_op jit(solution)/shard_map/pallas_call | solution.py:344
  121.2 0.9 copy.12
Async XLA Ops:
  0.0 0.7 copy-start.2
  0.7 0.7 copy-start.3
  0.7 0.7 copy-start.4
  1.3 1.1 copy-start
  2.5 0.7 copy-start.1

commit v4 on v3

--- a/solution.py
+++ b/solution.py
@@ -10,6 +10,7 @@
 CHUNKS = ((16, 32), (16, 32))
 BURST = 4
 SMALL = 16
+UNROLL = 8
 LANES = 128
 
 
@@ -55,7 +56,7 @@
     out,
     rows, sources, counts, lists, key, rank, order, source, keep, last_slot, filled,
     values, w_in, w_rec, bias, first0, first1, next0, next1, pack,
-    arrived00, arrived01, arrived10, arrived11, sums, mixed, inputs, hidden, final, gates,
+    arrived00, arrived01, arrived10, arrived11, sums, mixed, inputs, hidden, final, gates_even, gates_odd,
     small_sem, load_sem, slab_sem, ahead_sem, back_sem,
 ):
     time, slab = lax.axis_index("tm"), lax.axis_index("slab")
@@ -179,23 +180,15 @@
             + bias[layer : layer + 1, :]
         )
 
-    def project(layer, n):
-        size, start = CHUNKS[layer][n], starts[layer][n]
-        block = 8 * size
-
-        @pl.loop(0, times // 8)
-        def _(m):
-            part = pl.ds(pl.multiple_of(start + m * block, block), block)
-            gates[part, :] = projected(layer, part)
-
     def recur(layer, n, send=None):
         size = CHUNKS[layer][n]
 
-        def advance(t, state):
+        def advance(t, state, gate_inputs):
             before, memory = state
             part = rows_of(layer, n, t)
-            total = projected(layer, part) if size <= SMALL else gates[part, :]
-            total = total + jnp.dot(before, w_rec[layer], preferred_element_type=jnp.float32)
+            total = gate_inputs + jnp.dot(
+                before, w_rec[layer], preferred_element_type=jnp.float32
+            )
             in_gate, forget, candidate, out_gate = (
                 total[:, k * units : (k + 1) * units] for k in range(4)
             )
@@ -208,24 +201,47 @@
                     hidden[half, part, :] = after[:, half * LANES : (half + 1) * LANES]
             return after, memory
 
+        def step(t, state):
+            return advance(t, state, projected(layer, rows_of(layer, n, t)))
+
         zero = (jnp.zeros((size, units), jnp.bfloat16), jnp.zeros((size, units), jnp.float32))
-        if send is None:
-            lax.fori_loop(0, times, advance, zero, unroll=8)
+        if size <= SMALL and send is None:
+            lax.fori_loop(0, times, step, zero, unroll=UNROLL)
             return
 
-        def burst(m, state):
+        bursts = times // BURST
+        block = BURST * size
+
+        def project(m, target):
+            start = starts[layer][n] + jnp.minimum(m, bursts - 1) * block
+            target[0:block, :] = projected(layer, pl.ds(pl.multiple_of(start, block), block))
+
+        def burst(m, state, ready):
             for k in range(BURST):
-                state = advance(m * BURST + k, state)
-            for k in range(1, BURST):
-                send(m * BURST + lax.rem(time + k, BURST))
-
-            @pl.when(m != time // BURST)
-            def _():
-                send(m * BURST + lax.rem(time, BURST))
+                if size <= SMALL:
+                    state = step(m * BURST + k, state)
+                else:
+                    state = advance(m * BURST + k, state, ready[k * size : (k + 1) * size, :])
+            if send is not None:
+                for k in range(1, BURST):
+                    send(m * BURST + lax.rem(time + k, BURST))
+
+                @pl.when(m != time // BURST)
+                def _():
+                    send(m * BURST + lax.rem(time, BURST))
 
             return state
 
-        lax.fori_loop(0, times // BURST, burst, zero)
+        def two_bursts(m, state):
+            for at, (ready, coming) in enumerate([(gates_even, gates_odd), (gates_odd, gates_even)]):
+                if size > SMALL:
+                    project(2 * m + at + 1, coming)
+                state = burst(2 * m + at, state, ready)
+            return state
+
+        if size > SMALL:
+            project(jnp.int32(0), gates_even)
+        lax.fori_loop(0, bursts // 2, two_bursts, zero)
 
     def returned(layer, half):
         if layer == layers - 1:
@@ -291,8 +307,6 @@
         for n in range(parts[layer]):
             for half in range(halves):
                 bulk_wait(inputs.at[layer, half, peers_bytes(layer, n)], ahead_sem.at[layer, half, n, 1])
-            if CHUNKS[layer][n] > SMALL:
-                project(layer, n)
             if n < final_part:
                 recur(layer, n)
                 for half in back_halves:
@@ -324,6 +338,10 @@
                 for half in range(halves):
                     if n < parts[layer] - 1 or half > 0:
                         bulk_wait(hidden.at[half, peers_bytes(layer, n)], back_sem.at[layer, half, n, 0])
+
+
+def pinned(x):
+    return pltpu.with_memory_space_constraint(x, pltpu.HBM)
 
 
 def local(
@@ -365,7 +383,7 @@
             half_rows,
             pltpu.VMEM((halves, rows, LANES), jnp.bfloat16),
             pltpu.VMEM((rows, units), jnp.bfloat16),
-            pltpu.VMEM((rows, 4 * units), jnp.float32),
+            *[pltpu.VMEM((BURST * max(map(max, CHUNKS)), 4 * units), jnp.float32)] * 2,
             pltpu.SemaphoreType.DMA((4,)),
             pltpu.SemaphoreType.DMA((6,)),
             pltpu.SemaphoreType.DMA((layers, halves, 2)),
@@ -373,11 +391,13 @@
             pltpu.SemaphoreType.DMA((layers, halves, parts, 2)),
         ],
         compiler_params=pltpu.CompilerParams(
-            collective_id=0, has_side_effects=True, vmem_limit_bytes=52 << 20
+            collective_id=0, has_side_effects=True, vmem_limit_bytes=48 << 20
         ),
     )(
-        tile_rows, tile_sources, tile_counts, ref_lists,
-        features[0].reshape(row_tiles, tile, width), tile_values[0], w_input, w_hidden, bias,
+        *map(pinned, (tile_rows, tile_sources)),
+        tile_counts,
+        *map(pinned, (ref_lists, features[0].reshape(row_tiles, tile, width), tile_values[0])),
+        *map(pinned, (w_input, w_hidden, bias)),
     )
     return result.reshape(1, rows, units)
 

time: 123 us -> 121 us (0.984)
  local copies, waits for them, and re-layouts: 3.36 us -> 0.88 us
    unnamed x11 -> x1, local copies, waits for them, and re-layouts: 3.36 us -> 0.88 us
where the time goes in v4:
time: 121 us; the launch traced here: 119 us
  Pallas kernels  118 us (98%)
    pallas_call x1, Pallas kernels, local(): pl.pallas_call(functools.partial(kernel, times, slabs, refs), out_shape=j...  118 us

profile of v4, /device:TPU:1, one launch (start us, length us, event | category | flops | bytes accessed | tf_op | source)
XLA Modules:
  0.0 119.1 jit_solution(2655938291560559732)
XLA Ops:
  0.7 117.5 %shard_map.91 = bf16[12,128,256]{2,1,0:T(8,128)(2,1)S(1)} custom-call(s32[1,32]{1,0:T(1,128)} %rows_hbm.1, s32[1,32]{1,0:T(1,128)} %sources_hbm.1, s32[1,1]{1,0:T(1,128)S(6)} %copy.11.counts_hbm, s32[1,8,32]{2,1,0:T(8,128)} %lists_hbm.1, bf16[12,128,256]{2,1,0:T(8,128)(2,1)} %bitcast.5, bf16[32,128,128]{2,1,0:T(8,128)(2,1)} %bitcast.4, ...), custom_call_target="tpu_custom_call" | custom-call | tf_op jit(solution)/shard_map/pallas_call | solution.py:362
  118.2 0.9 copy.12

commit v5 on v4

--- a/solution.py
+++ b/solution.py
@@ -57,7 +57,7 @@
     rows, sources, counts, lists, key, rank, order, source, keep, last_slot, filled,
     values, w_in, w_rec, bias, first0, first1, next0, next1, pack,
     arrived00, arrived01, arrived10, arrived11, sums, mixed, inputs, hidden, final, gates_even, gates_odd,
-    small_sem, load_sem, slab_sem, ahead_sem, back_sem,
+    small_sem, load_sem, slab_sem, ahead_sem, plane_sem, back_sem,
 ):
     time, slab = lax.axis_index("tm"), lax.axis_index("slab")
     slots, row_tiles = key.shape[0], last_slot.shape[0]
@@ -158,13 +158,42 @@
         def _(step):
             send(lax.rem(time + step, times))
 
+    def far_first(send):
+        send(lax.rem(time + times // 2, times))
+
+        @pl.loop(1, times // 2)
+        def _(step):
+            send(lax.rem(time + times // 2 - step, times))
+            send(lax.rem(time + times // 2 + step, times))
+
+    def in_planes(half, n):
+        return half == halves - 1 and n == 0
+
+    def plane_wait(layer, m):
+        size, start = CHUNKS[layer][0], starts[layer][0]
+        near = time // BURST
+
+        @pl.when(m != near)
+        def _():
+            bulk_wait(inputs.at[layer, halves - 1, pl.ds(start, BURST * size)], plane_sem.at[layer, m])
+
+        @pl.when(m == near)
+        def _():
+            bulk_wait(
+                inputs.at[layer, halves - 1, pl.ds(start, (BURST - 1) * size)], plane_sem.at[layer, m]
+            )
+
     def send_ahead(layer, half, n):
         def send(peer):
             pltpu.make_async_remote_copy(
                 src_ref=mixed.at[layer, half, rows_of(layer, n, peer)],
                 dst_ref=inputs.at[layer, half, rows_of(layer, n, time)],
                 send_sem=ahead_sem.at[layer, half, n, 0],
-                recv_sem=ahead_sem.at[layer, half, n, 1],
+                recv_sem=(
+                    plane_sem.at[layer, time // BURST]
+                    if in_planes(half, n)
+                    else ahead_sem.at[layer, half, n, 1]
+                ),
                 device_id={"tm": peer},
             ).start()
 
@@ -205,6 +234,17 @@
             return advance(t, state, projected(layer, rows_of(layer, n, t)))
 
         zero = (jnp.zeros((size, units), jnp.bfloat16), jnp.zeros((size, units), jnp.float32))
+        if n == 0:
+
+            def plane(m, state):
+                plane_wait(layer, m)
+                for k in range(BURST):
+                    state = step(m * BURST + k, state)
+                return state
+
+            lax.fori_loop(0, times // BURST, plane, zero)
+            return
+
         if size <= SMALL and send is None:
             lax.fori_loop(0, times, step, zero, unroll=UNROLL)
             return
@@ -301,12 +341,15 @@
             slab_wait(layer, half, 1)
             add_slots(layer, half)
             for n in range(parts[layer]):
-                every_peer(send_ahead(layer, half, n))
+                (far_first if in_planes(half, n) else every_peer)(send_ahead(layer, half, n))
                 keep_own(layer, half, n)
 
         for n in range(parts[layer]):
             for half in range(halves):
-                bulk_wait(inputs.at[layer, half, peers_bytes(layer, n)], ahead_sem.at[layer, half, n, 1])
+                if not in_planes(half, n):
+                    bulk_wait(
+                        inputs.at[layer, half, peers_bytes(layer, n)], ahead_sem.at[layer, half, n, 1]
+                    )
             if n < final_part:
                 recur(layer, n)
                 for half in back_halves:
@@ -388,6 +431,7 @@
             pltpu.SemaphoreType.DMA((6,)),
             pltpu.SemaphoreType.DMA((layers, halves, 2)),
             pltpu.SemaphoreType.DMA((layers, halves, parts, 2)),
+            pltpu.SemaphoreType.DMA((layers, times // BURST)),
             pltpu.SemaphoreType.DMA((layers, halves, parts, 2)),
         ],
         compiler_params=pltpu.CompilerParams(

time: 121 us -> 118 us (0.975)
  Pallas kernels: 118 us -> 115 us
    pallas_call x1, Pallas kernels: 118 us -> 115 us  [local(): pl.pallas_call(functools.partial(kernel, times, slabs, refs), out_shape=j...]
where the time goes in v5:
time: 118 us; the launch traced here: 117 us
  Pallas kernels  115 us (97%)
    pallas_call x1, Pallas kernels, local(): pl.pallas_call(functools.partial(kernel, times, slabs, refs), out_shape=j...  115 us

profile of v5, /device:TPU:1, one launch (start us, length us, event | category | flops | bytes accessed | tf_op | source)
XLA Modules:
  0.0 116.9 jit_solution(15031894814626089691)
XLA Ops:
  0.7 115.4 %shard_map.91 = bf16[12,128,256]{2,1,0:T(8,128)(2,1)S(1)} custom-call(s32[1,32]{1,0:T(1,128)} %rows_hbm.1, s32[1,32]{1,0:T(1,128)} %sources_hbm.1, s32[1,1]{1,0:T(1,128)S(6)} %copy.11.counts_hbm, s32[1,8,32]{2,1,0:T(8,128)} %lists_hbm.1, bf16[12,128,256]{2,1,0:T(8,128)(2,1)} %bitcast.5, bf16[32,128,128]{2,1,0:T(8,128)(2,1)} %bitcast.4, ...), custom_call_target="tpu_custom_call" | custom-call | tf_op jit(solution)/shard_map/pallas_call | solution.py:405
  116.0 0.9 copy.12

commit v6 on v5

--- a/solution.py
+++ b/solution.py
@@ -10,7 +10,6 @@
 CHUNKS = ((16, 32), (16, 32))
 BURST = 4
 SMALL = 16
-UNROLL = 8
 LANES = 128
 
 
@@ -167,20 +166,22 @@
             send(lax.rem(time + times // 2 + step, times))
 
     def in_planes(half, n):
-        return half == halves - 1 and n == 0
-
-    def plane_wait(layer, m):
-        size, start = CHUNKS[layer][0], starts[layer][0]
+        return half == halves - 1
+
+    def plane_wait(layer, n, m):
+        size, start = CHUNKS[layer][n], starts[layer][n]
         near = time // BURST
 
         @pl.when(m != near)
         def _():
-            bulk_wait(inputs.at[layer, halves - 1, pl.ds(start, BURST * size)], plane_sem.at[layer, m])
+            bulk_wait(
+                inputs.at[layer, halves - 1, pl.ds(start, BURST * size)], plane_sem.at[layer, n, m]
+            )
 
         @pl.when(m == near)
         def _():
             bulk_wait(
-                inputs.at[layer, halves - 1, pl.ds(start, (BURST - 1) * size)], plane_sem.at[layer, m]
+                inputs.at[layer, halves - 1, pl.ds(start, (BURST - 1) * size)], plane_sem.at[layer, n, m]
             )
 
     def send_ahead(layer, half, n):
@@ -190,7 +191,7 @@
                 dst_ref=inputs.at[layer, half, rows_of(layer, n, time)],
                 send_sem=ahead_sem.at[layer, half, n, 0],
                 recv_sem=(
-                    plane_sem.at[layer, time // BURST]
+                    plane_sem.at[layer, n, time // BURST]
                     if in_planes(half, n)
                     else ahead_sem.at[layer, half, n, 1]
                 ),
@@ -234,10 +235,10 @@
             return advance(t, state, projected(layer, rows_of(layer, n, t)))
 
         zero = (jnp.zeros((size, units), jnp.bfloat16), jnp.zeros((size, units), jnp.float32))
-        if n == 0:
+        if size <= SMALL and send is None:
 
             def plane(m, state):
-                plane_wait(layer, m)
+                plane_wait(layer, n, m)
                 for k in range(BURST):
                     state = step(m * BURST + k, state)
                 return state
@@ -245,18 +246,17 @@
             lax.fori_loop(0, times // BURST, plane, zero)
             return
 
-        if size <= SMALL and send is None:
-            lax.fori_loop(0, times, step, zero, unroll=UNROLL)
-            return
-
         bursts = times // BURST
         block = BURST * size
 
         def project(m, target):
             start = starts[layer][n] + jnp.minimum(m, bursts - 1) * block
+            pl.when(m < bursts)(lambda: plane_wait(layer, n, m))
             target[0:block, :] = projected(layer, pl.ds(pl.multiple_of(start, block), block))
 
         def burst(m, state, ready):
+            if size <= SMALL:
+                plane_wait(layer, n, m)
             for k in range(BURST):
                 if size <= SMALL:
                     state = step(m * BURST + k, state)
@@ -431,7 +431,7 @@
             pltpu.SemaphoreType.DMA((6,)),
             pltpu.SemaphoreType.DMA((layers, halves, 2)),
             pltpu.SemaphoreType.DMA((layers, halves, parts, 2)),
-            pltpu.SemaphoreType.DMA((layers, times // BURST)),
+            pltpu.SemaphoreType.DMA((layers, parts, times // BURST)),
             pltpu.SemaphoreType.DMA((layers, halves, parts, 2)),
         ],
         compiler_params=pltpu.CompilerParams(

time: 118 us -> 118 us (level)
  no operation moved by 1% of the time
where the time goes in v6:
time: 118 us; the launch traced here: 117 us
  Pallas kernels  115 us (97%)
    pallas_call x1, Pallas kernels, local(): pl.pallas_call(functools.partial(kernel, times, slabs, refs), out_shape=j...  115 us

profile of v6, /device:TPU:1, one launch (start us, length us, event | category | flops | bytes accessed | tf_op | source)
XLA Modules:
  0.0 116.9 jit_solution(1470328030559477142)
XLA Ops:
  0.7 115.3 %shard_map.91 = bf16[12,128,256]{2,1,0:T(8,128)(2,1)S(1)} custom-call(s32[1,32]{1,0:T(1,128)} %rows_hbm.1, s32[1,32]{1,0:T(1,128)} %sources_hbm.1, s32[1,1]{1,0:T(1,128)S(6)} %copy.11.counts_hbm, s32[1,8,32]{2,1,0:T(8,128)} %lists_hbm.1, bf16[12,128,256]{2,1,0:T(8,128)(2,1)} %bitcast.5, bf16[32,128,128]{2,1,0:T(8,128)(2,1)} %bitcast.4, ...), custom_call_target="tpu_custom_call" | custom-call | tf_op jit(solution)/shard_map/pallas_call | solution.py:405
  116.0 0.9 copy.12

commit v7 on v6

--- a/solution.py
+++ b/solution.py
@@ -350,7 +350,7 @@
                     bulk_wait(
                         inputs.at[layer, half, peers_bytes(layer, n)], ahead_sem.at[layer, half, n, 1]
                     )
-            if n < final_part:
+            if n < final_part and layer < layers - 1:
                 recur(layer, n)
                 for half in back_halves:
                     every_peer(send_back(layer, half, n))

time: 118 us -> 117 us (level)
  no operation moved by 1% of the time
where the time goes in v7:
time: 117 us
  Pallas kernels  115 us (98%)
    pallas_call x1, Pallas kernels, local(): pl.pallas_call(functools.partial(kernel, times, slabs, refs), out_shape=j...  115 us

profile of v7, /device:TPU:1, one launch (start us, length us, event | category | flops | bytes accessed | tf_op | source)
XLA Modules:
  0.0 116.9 jit_solution(3919826547752342430)
XLA Ops:
  0.7 115.3 %shard_map.91 = bf16[12,128,256]{2,1,0:T(8,128)(2,1)S(1)} custom-call(s32[1,32]{1,0:T(1,128)} %rows_hbm.1, s32[1,32]{1,0:T(1,128)} %sources_hbm.1, s32[1,1]{1,0:T(1,128)S(6)} %copy.11.counts_hbm, s32[1,8,32]{2,1,0:T(8,128)} %lists_hbm.1, bf16[12,128,256]{2,1,0:T(8,128)(2,1)} %bitcast.5, bf16[32,128,128]{2,1,0:T(8,128)(2,1)} %bitcast.4, ...), custom_call_target="tpu_custom_call" | custom-call | tf_op jit(solution)/shard_map/pallas_call | solution.py:405
  116.0 0.9 copy.12
